TPU v7x, 32 devices: a whole 2x2x4 slice. The times are simulated.
32 devices in a mesh: grp: 4 (over y, x), space: 8 (over z, core).
Axes of the slice: x: 2, y: 2, z: 4, core: 2. Of those that a mesh axis runs over, the one named last changes fastest.
Arguments:
- features: bfloat16 [4, 128, 128, 128], P('grp', 'space'), may hold values from -6 to 6
- weights: bfloat16 [27, 128, 128], replicated, may hold values from -0.109375 to 0.109375
- cotangent: bfloat16 [4, 128, 128, 128], P('grp', 'space'), may hold values from -6 to 6
- kernel_map: int32 [4, 128, 27], P('grp', 'space'), may hold values from -1 to 127, as said below
- counts: int32 [4, 8], P('grp', 'space'), may hold values from 4 to 16
Outputs:
- output: bfloat16 [4, 128, 128, 128], P('grp', 'space')
- input_grad: bfloat16 [4, 128, 128, 128], P('grp', 'space')
- weight_grad: float32 [3456, 128], P('space')
Inputs may be any that keep to these rules, and one draw needn't show every extreme that they name: `kernel_map`: the centre offset k = 27 div 2 maps every block to itself. Otherwise an entry for an output block b on slab d = b div 16 is -1 or lies in [d * 16 - 4, (d + 1) * 16 + 4) within the sample. The live blocks of a device are its first counts slots.
All inputs are finite; a program needn't handle non-finite values.
Results may differ from a plain program's by a relative error of at most 0.005.
Values may be sent and summed in bfloat16 or wider, within the bound.
A program may use at most 64 MiB of HBM per device.

v0:
```python
import jax
import jax.numpy as jnp
from jax import lax
from jax.sharding import PartitionSpec as P

K = 27
H = 4


def extended_2(block, sides, width):
    for axis, dim in sides:
        count = lax.axis_size(axis)
        forward = [(i, i + 1) for i in range(count - 1)]
        backward = [(target, source) for source, target in forward]
        low = lax.ppermute(
            lax.slice_in_dim(block, block.shape[dim] - width, None, axis=dim), axis, forward
        )
        high = lax.ppermute(lax.slice_in_dim(block, 0, width, axis=dim), axis, backward)
        block = jnp.concatenate([low, block, high], axis=dim)
    return block


def passed_along(block, axis, distance):
    devices = range(lax.axis_size(axis))
    route = [(i - distance, i) for i in devices if i - distance in devices]
    return lax.ppermute(block, axis, route)


def per_device(features, weights, cotangent, kernel_map, counts):
    voxels = features[0]
    slots = voxels.shape[0]
    device = lax.axis_index("space")
    live_mask = (jnp.arange(slots) < counts[0, 0]).astype(jnp.bfloat16)[:, None, None]
    live_float = live_mask.astype(jnp.float32)
    masked = voxels * live_mask
    grad_out = cotangent[0] * live_mask
    extended = extended_2(masked, (("space", 0),), H)
    block_map = kernel_map[0]
    first_block = device * slots - H
    present = (block_map >= 0).astype(jnp.bfloat16)
    local_index = jnp.where(block_map >= 0, block_map - first_block, 0)
    channels_in = voxels.shape[2]
    channels_out = weights.shape[2]

    def step(offset, carry):
        total, grad_in, wgrad = carry
        column = lax.dynamic_index_in_dim(local_index, offset, 1, keepdims=False)
        present_k = lax.dynamic_index_in_dim(present, offset, 1, keepdims=False)[:, None, None]
        gathered = jnp.take(extended, column, axis=0) * present_k
        kernel = lax.dynamic_index_in_dim(weights, offset, 0, keepdims=False)
        total = total + jnp.einsum(
            "brc,co->bro", gathered, kernel, preferred_element_type=jnp.float32
        )
        term = jnp.einsum("bro,co->brc", grad_out, kernel, preferred_element_type=jnp.float32)
        grad_in = grad_in.at[column].add(term * present_k.astype(jnp.float32))
        piece = jnp.einsum("brc,bro->co", gathered, grad_out, preferred_element_type=jnp.float32)
        wgrad = lax.dynamic_update_index_in_dim(wgrad, piece, offset, 0)
        return (total, grad_in, wgrad)

    start = (
        jnp.zeros((slots, voxels.shape[1], channels_out), jnp.float32),
        jnp.zeros((slots + 2 * H, voxels.shape[1], channels_in), jnp.float32),
        jnp.zeros((K, channels_in, channels_out), jnp.float32),
    )
    total, grad_in, wgrad = lax.fori_loop(0, K, step, start)
    output = (total * live_float).astype(jnp.bfloat16)
    lower_rim = grad_in[:H]
    upper_rim = grad_in[slots + H :]
    own_grad = grad_in[H : slots + H]
    from_above = passed_along(lower_rim.astype(jnp.bfloat16), "space", -1).astype(lower_rim.dtype)
    from_below = passed_along(upper_rim.astype(jnp.bfloat16), "space", 1).astype(upper_rim.dtype)
    own_grad = own_grad.at[:H].add(from_below)
    own_grad = own_grad.at[slots - H :].add(from_above)
    input_grad = (own_grad * live_float).astype(jnp.bfloat16)
    weight_rows = wgrad.reshape(K * channels_in, channels_out)
    summed = lax.psum(weight_rows, ("grp", "space"))
    row_count = weight_rows.shape[0] // lax.axis_size("space")
    own_rows = lax.dynamic_slice_in_dim(summed, device * row_count, row_count, 0)
    return (output[None], input_grad[None], own_rows)


def solution(mesh):
    in_specs = (
        P("grp", "space", None, None),
        P(),
        P("grp", "space", None, None),
        P("grp", "space", None),
        P("grp", "space"),
    )
    out_specs = (P("grp", "space", None, None), P("grp", "space", None, None), P("space", None))
    return jax.shard_map(
        per_device, mesh=mesh, in_specs=in_specs, out_specs=out_specs, check_vma=False
    )
```

profile of v0, /device:TPU:0, one launch (start us, length us, event | category | flops | bytes accessed | tf_op | source)
XLA Modules:
  0.0 446.6 jit_solution(6604111132095993957)
XLA Ops:
  13.1 4.0 collective-permute-done.1
  19.4 278.4 %while.20 = (s32[]{:T(128)}, f32[16,128,128]{2,1,0:T(8,128)}, f32[24,128,128]{2,1,0:T(8,128)}, f32[27,128,128]{2,1,0:T(8,128)}, s32[16,27]{0,1:T(8,128)S(1)}, /*...) while((s32[]{:T(128)}, f32[16,128,128]{2,1,0:T(8,128)}, ...), condition=%wide.region_2.3_spmd.clone, body=%wide.region_0.2_spmd.clone.sunk | while | flops 203424880 | bytes 11670275 | solution.py:65
  24.7 3.5 scatter_fusion
  35.2 3.4 scatter_fusion
  45.6 3.3 scatter_fusion
  51.9 2.6 convolution_add_fusion.2
  55.9 3.4 scatter_fusion
  66.3 3.3 scatter_fusion
  76.6 3.3 scatter_fusion
  86.9 3.3 scatter_fusion
  97.1 3.4 scatter_fusion
  107.5 3.3 scatter_fusion
  117.8 3.3 scatter_fusion
  128.1 3.3 scatter_fusion
  138.3 3.4 scatter_fusion
  148.7 3.3 scatter_fusion
  158.9 3.4 scatter_fusion
  169.3 3.3 scatter_fusion
  179.6 3.4 scatter_fusion
  189.9 3.4 scatter_fusion
  200.3 3.4 scatter_fusion
  210.6 3.4 scatter_fusion
  220.9 3.4 scatter_fusion
  231.2 3.4 scatter_fusion
  241.6 3.3 scatter_fusion
  251.9 3.4 scatter_fusion
  262.3 3.3 scatter_fusion
  272.6 3.4 scatter_fusion
  282.9 3.3 scatter_fusion
  293.2 3.4 scatter_fusion
  299.4 6.2 %collective-permute-start.2 = (bf16[4,128,128]{2,1,0:T(8,128)(2,1)S(1)}, bf16[4,128,128]{2,1,0:T(8,128)(2,1)S(1)}, u32[]{:S(2)}, u32[]{:S(2)}) collective-permute-start(bf16[4,128,128]{2,1,0:T(8,128)(2,1)S(1)} %get-tuple-element.239), channel_id=1, source_target_pairs={{0,1},{1,2},{2,3},{3,4},{4,5},{5,6},{6,7},{8,9},{9,10},{10,11},{11... | collective-permute-start | bytes 393224 | tf_op jit(solution)/shard_map/ppermute | solution.py:26
  311.6 126.6 %all-reduce.2.cloned.1.call-done = f32[3456,128]{1,0:T(8,128)} async-done(((f32[3456,128]{1,0:T(8,128)}), f32[3456,128]{1,0:T(8,128)}) %all-reduce.2.cloned.1.call-update) | async-done | bytes 1769488 | tf_op jit(solution)/shard_map/psum | solution.py:76
  (245 shorter events, 200.7 us)
Async XLA Ops:
  7.2 5.8 %copy-start.1 = (s32[1,16,27]{2,1,0:T(8,128)S(1)}, s32[1,16,27]{2,1,0:T(8,128)}, u32[]{:S(2)}) copy-start(s32[1,16,27]{2,1,0:T(8,128)} %param.14) | copy-start | bytes 5188
  7.2 431.0 %all-reduce.2.cloned.1.call-start = ((), (), s32[]{:S(2)}) async-start(), calls=%async_computation | async-start | bytes 3538944 | tf_op jit(solution)/shard_map/psum | solution.py:76
  9.2 3.8 collective-permute-start
  11.7 5.4 %collective-permute-start.1 = (bf16[4,128,128]{2,1,0:T(8,128)(2,1)S(1)}, bf16[4,128,128]{2,1,0:T(8,128)(2,1)S(1)}, u32[]{:S(2)}, u32[]{:S(2)}) collective-permute-start(bf16[4,128,128]{2,1,0:T(8,128)(2,1)S(1)} %get-tuple-element.241), channel_id=1, source_target_pairs={{1,0},{2,1},{3,2},{4,3},{5,4},{6,5},{7,6},{9,8},{10,9},{11,10},{12... | collective-permute-start | bytes 393224 | tf_op jit(solution)/shard_map/ppermute | solution.py:18
  297.7 7.9 %copy-start = (f32[24,128,128]{2,1,0:T(8,128)S(1)}, f32[24,128,128]{2,1,0:T(8,128)}, u32[]{:S(2)}) copy-start(f32[24,128,128]{2,1,0:T(8,128)} %get-tuple-element.184) | copy-start | bytes 4718596
  299.4 7.6 %collective-permute-start.2 = (bf16[4,128,128]{2,1,0:T(8,128)(2,1)S(1)}, bf16[4,128,128]{2,1,0:T(8,128)(2,1)S(1)}, u32[]{:S(2)}, u32[]{:S(2)}) collective-permute-start(bf16[4,128,128]{2,1,0:T(8,128)(2,1)S(1)} %get-tuple-element.239), channel_id=1, source_target_pairs={{0,1},{1,2},{2,3},{3,4},{4,5},{5,6},{6,7},{8,9},{9,10},{10,11},{11... | collective-permute-start | bytes 393224 | tf_op jit(solution)/shard_map/ppermute | solution.py:26
  305.8 3.2 collective-permute-start.3
Sparse Core Ops, SparseCore 0:
  305.8 132.3 all-reduce.1
where the time goes:
time: 453 us; the launch traced here: 447 us
  waiting for transfers between devices  132 us (29%)
  matrix products  129 us (28%)
  other arithmetic  98.1 us (22%)
  local copies, waits for them, and re-layouts  60.2 us (13%)
  between operations  14.8 us (3%)
  starting transfers between devices  11.2 us (2%)
    psum x1, waiting for transfers between devices, per_device(): summed = lax.psum(weight_rows, ('grp', 'space'))  127 us
    scatter-add x27, other arithmetic, step(): grad_in = grad_in.at[column].add(term * present_k.astype(jnp.float32))  90.8 us
    dot_general x27, matrix products, step(): jnp.einsum('brc,co->bro', gathered, kernel, preferred_element_type=jnp.fl...  70 us
    gather x27, local copies, waits for them, and re-layouts, step(): gathered = jnp.take(extended, column, axis=0) * present_k  48.1 us
    dot_general x27, matrix products, step(): jnp.einsum('brc,bro->co', gathered, grad_out, preferred_element_type=jnp....  30.5 us
    dot_general x27, matrix products, step(): jnp.einsum('bro,co->brc', grad_out, kernel, preferred_element_type=jnp.fl...  28.4 us
  transfers between devices with their start and end apart: 5, of which 3 were waited for; matrix products, arithmetic and copies ran while one was open for 1% of the time, Pallas kernels for 0%

commit v1 on v0

--- a/solution.py
+++ b/solution.py
@@ -73,7 +73,8 @@
     own_grad = own_grad.at[slots - H :].add(from_above)
     input_grad = (own_grad * live_float).astype(jnp.bfloat16)
     weight_rows = wgrad.reshape(K * channels_in, channels_out)
-    summed = lax.psum(weight_rows, ("grp", "space"))
+    half = lax.psum(weight_rows, "space")
+    summed = lax.psum(half, "grp")
     row_count = weight_rows.shape[0] // lax.axis_size("space")
     own_rows = lax.dynamic_slice_in_dim(summed, device * row_count, row_count, 0)
     return (output[None], input_grad[None], own_rows)

time: 453 us -> 446 us (0.985)
  starting transfers between devices: 11.2 us -> 6.36 us
    ppermute x2, starting transfers between devices: 7.46 us -> 2.59 us  [passed_along(): return lax.ppermute(block, axis, route)]
    psum x1 -> x2, waiting for transfers between devices: 127 us -> 125 us  [the longest x1 66.9 us: per_device(): half = lax.psum(weight_rows, 'space')]
  transfers between devices with their start and end apart: 5 -> 6, of which waited for: 3 -> 4; matrix products, arithmetic and copies ran while one was open for 1% -> 1% of each run, Pallas kernels for 0% -> 0%
where the time goes in v1:
time: 446 us; the launch traced here: 440 us
  waiting for transfers between devices  132 us (30%)
  matrix products  129 us (29%)
  other arithmetic  96.6 us (22%)
  local copies, waits for them, and re-layouts  60.2 us (13%)
  between operations  14.9 us (3%)
  starting transfers between devices  6.36 us (1%)
    scatter-add x27, other arithmetic, step(): grad_in = grad_in.at[column].add(term * present_k.astype(jnp.float32))  90.8 us
    dot_general x27, matrix products, step(): jnp.einsum('brc,co->bro', gathered, kernel, preferred_element_type=jnp.fl...  70 us
    psum x1, waiting for transfers between devices, per_device(): half = lax.psum(weight_rows, 'space')  66.9 us
    psum x1, waiting for transfers between devices, per_device(): summed = lax.psum(half, 'grp')  58.1 us
    gather x27, local copies, waits for them, and re-layouts, step(): gathered = jnp.take(extended, column, axis=0) * present_k  48.1 us
    dot_general x27, matrix products, step(): jnp.einsum('brc,bro->co', gathered, grad_out, preferred_element_type=jnp....  30.5 us
    dot_general x27, matrix products, step(): jnp.einsum('bro,co->brc', grad_out, kernel, preferred_element_type=jnp.fl...  28.4 us
    mul x27, local copies, waits for them, and re-layouts, step(): grad_in = grad_in.at[column].add(term * present_k.astype(jnp.float32))  8.94 us
  transfers between devices with their start and end apart: 6, of which 4 were waited for; matrix products, arithmetic and copies ran while one was open for 1% of the time, Pallas kernels for 0%

profile of v1, /device:TPU:0, one launch (start us, length us, event | category | flops | bytes accessed | tf_op | source)
XLA Modules:
  0.0 439.7 jit_solution(11190660362098154049)
XLA Ops:
  13.1 4.0 collective-permute-done.1
  19.4 278.4 %while.20 = (s32[]{:T(128)}, f32[16,128,128]{2,1,0:T(8,128)}, f32[24,128,128]{2,1,0:T(8,128)}, f32[27,128,128]{2,1,0:T(8,128)}, s32[16,27]{0,1:T(8,128)S(1)}, /*...) while((s32[]{:T(128)}, f32[16,128,128]{2,1,0:T(8,128)}, ...), condition=%wide.region_2.3_spmd.clone, body=%wide.region_0.2_spmd.clone.sunk | while | flops 203424880 | bytes 11670275 | solution.py:65
  24.7 3.5 scatter_fusion
  35.2 3.4 scatter_fusion
  45.6 3.3 scatter_fusion
  55.9 3.4 scatter_fusion
  66.3 3.3 scatter_fusion
  76.6 3.3 scatter_fusion
  86.9 3.3 scatter_fusion
  97.1 3.4 scatter_fusion
  107.5 3.3 scatter_fusion
  117.8 3.3 scatter_fusion
  128.1 3.3 scatter_fusion
  138.3 3.4 scatter_fusion
  148.7 3.3 scatter_fusion
  158.9 3.4 scatter_fusion
  169.3 3.3 scatter_fusion
  179.6 3.4 scatter_fusion
  189.9 3.4 scatter_fusion
  200.3 3.4 scatter_fusion
  210.6 3.4 scatter_fusion
  220.9 3.4 scatter_fusion
  231.2 3.4 scatter_fusion
  241.6 3.3 scatter_fusion
  251.9 3.4 scatter_fusion
  262.3 3.3 scatter_fusion
  272.6 3.4 scatter_fusion
  282.9 3.3 scatter_fusion
  293.2 3.4 scatter_fusion
  297.8 66.9 %all-reduce.3.cloned.1.call-done = f32[3456,128]{1,0:T(8,128)} async-done(((f32[3456,128]{1,0:T(8,128)}), f32[3456,128]{1,0:T(8,128)}) %all-reduce.3.cloned.1.call-update) | async-done | bytes 1769488 | tf_op jit(solution)/shard_map/psum | solution.py:76
  367.7 2.9 collective-permute-done.3
  373.1 58.1 %all-reduce.5.cloned.1.call-done = f32[3456,128]{1,0:T(8,128)} async-done(((f32[3456,128]{1,0:T(8,128)}), f32[3456,128]{1,0:T(8,128)}) %all-reduce.5.cloned.1.call-update) | async-done | bytes 1769488 | tf_op jit(solution)/shard_map/psum | solution.py:77
  (248 shorter events, 201.2 us)
Async XLA Ops:
  7.2 5.8 %copy-start.1 = (s32[1,16,27]{2,1,0:T(8,128)S(1)}, s32[1,16,27]{2,1,0:T(8,128)}, u32[]{:S(2)}) copy-start(s32[1,16,27]{2,1,0:T(8,128)} %param.14) | copy-start | bytes 5188
  7.2 357.6 %all-reduce.3.cloned.1.call-start = ((), (), s32[]{:S(2)}) async-start(), calls=%async_computation | async-start | bytes 3538944 | tf_op jit(solution)/shard_map/psum | solution.py:76
  9.2 3.8 collective-permute-start
  11.7 5.4 %collective-permute-start.1 = (bf16[4,128,128]{2,1,0:T(8,128)(2,1)S(1)}, bf16[4,128,128]{2,1,0:T(8,128)(2,1)S(1)}, u32[]{:S(2)}, u32[]{:S(2)}) collective-permute-start(bf16[4,128,128]{2,1,0:T(8,128)(2,1)S(1)} %get-tuple-element.241), channel_id=1, source_target_pairs={{1,0},{2,1},{3,2},{4,3},{5,4},{6,5},{7,6},{9,8},{10,9},{11,10},{12... | collective-permute-start | bytes 393224 | tf_op jit(solution)/shard_map/ppermute | solution.py:18
  297.7 67.0 %copy-start = (f32[24,128,128]{2,1,0:T(8,128)S(1)}, f32[24,128,128]{2,1,0:T(8,128)}, u32[]{:S(2)}) copy-start(f32[24,128,128]{2,1,0:T(8,128)} %get-tuple-element.184) | copy-start | bytes 4718596
  297.8 133.4 %all-reduce.5.cloned.1.call-start = ((), (), s32[]{:S(2)}) async-start(), calls=%async_computation.1 | async-start | bytes 3538944 | tf_op jit(solution)/shard_map/psum | solution.py:77
  364.9 2.7 collective-permute-start.2
  366.3 4.2 collective-permute-start.3
Sparse Core Ops, SparseCore 0:
  297.9 66.7 all-reduce.2
  367.9 63.2 all-reduce.4
